TPU v7x, 32 devices: a whole 2x2x4 slice. The times are simulated.
32 devices in a mesh: dom: 8 (over z, y), sub: 4 (over x, core).
Axes of the slice: x: 2, y: 2, z: 4, core: 2. Of those that a mesh axis runs over, the one named last changes fastest.
Arguments:
- fine_latent: bfloat16 [1024, 64, 128], P(('dom', 'sub')), may hold values from -6 to 6
- coarse_latent: bfloat16 [256, 64, 128], P(('dom', 'sub')), may hold values from -6 to 6
- adj_index: int32 [1024, 16], P(('dom', 'sub')), may hold values from 0 to 63
- adj_weight: bfloat16 [1024, 64, 1024], P(('dom', 'sub')), may hold values from -0.1875 to 0.1875
- interp_slot: int32 [1024, 4], P(('dom', 'sub')), may hold values from 0 to 31
- interp_weight: bfloat16 [1024, 64, 256], P(('dom', 'sub')), may hold values from -0.375 to 0.375
- coarse_send: int32 [32, 32, 1], P(('dom', 'sub')), may hold values from 0 to 7
- halo_sub_send: int32 [32, 4, 4], P(('dom', 'sub')), may hold values from 0 to 31
- halo_dom_send: int32 [32, 2, 8], P(('dom', 'sub')), may hold values from 0 to 31
- block_count: int32 [32], P(('dom', 'sub')), may hold values from 16 to 32, as said below
- w_in: bfloat16 [2, 384, 128], replicated, may hold values from -0.3125 to 0.3125
- b_in: float32 [2, 128], replicated, may hold values from -3 to 3
- w_out: bfloat16 [2, 128, 128], replicated, may hold values from -0.5 to 0.5
- ln_gain: float32 [2, 128], replicated, may hold values from 0.25 to 1.75
Outputs:
- fine_out: bfloat16 [1024, 64, 128], P(('dom', 'sub'))
Inputs may be any that keep to these rules, and one draw needn't show every extreme that they name: `block_count`: some device has all 32 blocks live and some has half of them.
All inputs are finite; a program needn't handle non-finite values.
Results may differ from a plain program's by a relative error of at most 0.0058.
Values may be sent and summed in bfloat16 or wider, within the bound.
A program may use at most 64 MiB of HBM per device.

v0:
```python
import functools
import math

import jax
import jax.numpy as jnp
from jax import lax
from jax.experimental import pallas as pl
from jax.experimental.pallas import tpu as pltpu
from jax.sharding import PartitionSpec as P

MESH = pl.DeviceIdType.MESH


def kernel(
    n_dom,
    n_sub,
    steps,
    adj_index,
    interp_slot,
    coarse_send,
    halo_sub_send,
    halo_dom_send,
    block_count,
    fine_hbm,
    coarse_hbm,
    adj_hbm,
    interp_hbm,
    w_in_hbm,
    b_in_hbm,
    w_out_hbm,
    ln_gain_hbm,
    out_hbm,
    *scratch,
):
    held = scratch[:steps]
    pools = scratch[steps : 2 * steps]
    sub_outs = scratch[2 * steps : 3 * steps]
    dom_outs = scratch[3 * steps : 4 * steps]
    (
        coarse,
        adj,
        iw,
        coarse_out,
        received,
        interp,
        summed,
        w_in,
        b_in,
        w_out,
        ln_gain,
        load_sem,
        out,
        out_sem,
        c_send,
        c_recv,
        s_send,
        s_recv,
        d_send,
        d_recv,
    ) = scratch[4 * steps :]

    n = n_dom * n_sub
    dom, sub = lax.axis_index("dom"), lax.axis_index("sub")
    me = dom * n_sub + sub
    n_fine, rows, lat = out_hbm.shape
    slots = coarse_out.shape[1]
    hs = sub_outs[0].shape[1]
    hd = dom_outs[0].shape[1]
    k_a, k_i = adj_index.shape[0], interp_slot.shape[0]

    barrier = pltpu.get_barrier_semaphore()

    def wrapped(position, size):
        return jnp.where(position >= size, position - size, position)

    subs = [wrapped(sub + o, n_sub) for o in range(n_sub)]
    ways = sorted(range(1, n_dom), key=lambda o: abs(o - n_dom // 2))

    def peers(act):
        for o in ways + [0]:
            to = wrapped(dom + o, n_dom)
            for other in subs[1:] if o == 0 else subs:
                act(to, other)

    def greet(to, other):
        pl.semaphore_signal(barrier, inc=1, device_id=(to, other), device_id_type=MESH)

    peers(greet)

    loads = [
        pltpu.make_async_copy(src, dst, load_sem.at[i])
        for i, (src, dst) in enumerate(
            [
                (fine_hbm, held[0]),
                (coarse_hbm, coarse),
                (adj_hbm, adj),
                (interp_hbm, iw),
                (w_in_hbm, w_in),
                (b_in_hbm, b_in),
                (w_out_hbm, w_out),
                (ln_gain_hbm, ln_gain),
            ]
        )
    ]
    for copy in loads:
        copy.start()

    def gather_sub(t):
        for i in range(n_sub):
            for s in range(hs):
                sub_outs[t][i, s] = held[t][halo_sub_send[0, i, s]]

    def gather_dom(t):
        for i in range(2):
            for s in range(hd):
                dom_outs[t][i, s] = held[t][halo_dom_send[0, i, s]]

    def sub_copy(t, peer, owner):
        return pltpu.make_async_remote_copy(
            src_ref=sub_outs[t].at[peer],
            dst_ref=pools[t].at[pl.ds(n_fine + owner * hs, hs)],
            send_sem=s_send.at[t, peer],
            recv_sem=s_recv.at[t, owner],
            device_id=(dom, peer),
            device_id_type=MESH,
        )

    def dom_copy(t, way):
        target = dom + 1 if way == 0 else dom - 1
        return pltpu.make_async_remote_copy(
            src_ref=dom_outs[t].at[way],
            dst_ref=pools[t].at[pl.ds(n_fine + n_sub * hs + way * hd, hd)],
            send_sem=d_send.at[t, way],
            recv_sem=d_recv.at[t, way],
            device_id=(target, sub),
            device_id_type=MESH,
        )

    def coarse_copy(to, other, owner):
        peer = to * n_sub + other
        return pltpu.make_async_remote_copy(
            src_ref=coarse_out.at[peer],
            dst_ref=received.at[pl.ds(owner * slots, slots)],
            send_sem=c_send.at[peer],
            recv_sem=c_recv.at[owner],
            device_id=(to, other),
            device_id_type=MESH,
        )

    def start_dom(t):
        @pl.when(dom < n_dom - 1)
        def _():
            dom_copy(t, 0).start()

        @pl.when(dom > 0)
        def _():
            dom_copy(t, 1).start()

    def start_sub(t):
        for o in range(1, n_sub):
            sub_copy(t, subs[o], sub).start()

    def local_pool(t):
        pools[t][pl.ds(n_fine + sub * hs, hs)] = sub_outs[t][sub]
        base = n_fine + n_sub * hs

        @pl.when(dom == 0)
        def _():
            pools[t][pl.ds(base, hd)] = jnp.zeros((hd, rows, lat), pools[t].dtype)

        @pl.when(dom == n_dom - 1)
        def _():
            pools[t][pl.ds(base + hd, hd)] = jnp.zeros((hd, rows, lat), pools[t].dtype)

    def wait_halo(t):
        for o in range(1, n_sub):
            owner = subs[o]
            sub_copy(t, owner, owner).wait_recv()

        @pl.when(dom > 0)
        def _():
            dom_copy(t, 0).wait_recv()

        @pl.when(dom < n_dom - 1)
        def _():
            dom_copy(t, 1).wait_recv()

    def finish_halo_sends(t):
        for o in range(1, n_sub):
            sub_copy(t, subs[o], sub).wait_send()

        @pl.when(dom < n_dom - 1)
        def _():
            dom_copy(t, 0).wait_send()

        @pl.when(dom > 0)
        def _():
            dom_copy(t, 1).wait_send()

    loads[0].wait()
    gather_dom(0)
    gather_sub(0)
    loads[1].wait()

    def gather_coarse(d, _):
        for s in range(slots):
            coarse_out[d, s] = coarse[coarse_send[0, s, d]]
        return 0

    lax.fori_loop(0, n, gather_coarse, 0)

    pl.semaphore_wait(barrier, n - 1)
    start_dom(0)
    start_sub(0)

    peers(lambda to, other: coarse_copy(to, other, me).start())

    received[pl.ds(me * slots, slots)] = coarse_out[me]
    pools[0][pl.ds(0, n_fine)] = held[0][...]
    local_pool(0)

    group = math.gcd(n_fine, 16)

    def product(weights, table, index, tiles, into):
        def body(g, _):
            for u in range(group):
                b = g * group + u
                picked = jnp.concatenate([table[index[k, b]] for k in range(tiles)], axis=0)
                into[b] = jnp.dot(
                    weights[b], picked, preferred_element_type=jnp.float32
                ).astype(into.dtype)
            return 0

        lax.fori_loop(0, n_fine // group, body, 0)

    chunk = math.gcd(n_fine, 32)
    live = block_count[0, 0]

    def stored(c):
        at = pl.ds(c * chunk, chunk)
        return pltpu.make_async_copy(out.at[at], out_hbm.at[at], out_sem.at[c])

    for t in range(steps):
        wait_halo(t)
        if t == 0:
            loads[2].wait()
        product(adj, pools[t], adj_index, k_a, summed)
        if t == 0:
            peers(lambda to, other: coarse_copy(to, other, to * n_sub + other).wait_recv())
            for copy in loads[3:]:
                copy.wait()
            product(iw, received, interp_slot, k_i, interp)

        wide = w_out[t].astype(jnp.float32)
        wide = wide - jnp.mean(wide, axis=-1, keepdims=True)
        high = wide.astype(jnp.bfloat16)
        low = (wide - high.astype(jnp.float32)).astype(jnp.bfloat16)
        split = jnp.concatenate([high, low], axis=1)
        ones = jnp.ones((lat, lat), jnp.bfloat16)

        def update(c, _):
            at = pl.ds(c * chunk, chunk)
            h = held[t][at].reshape(chunk * rows, lat)
            joined = jnp.concatenate(
                [
                    h,
                    summed[at].reshape(chunk * rows, lat),
                    interp[at].reshape(chunk * rows, lat),
                ],
                axis=1,
            )
            hidden = jnp.dot(joined, w_in[t], preferred_element_type=jnp.float32)
            hidden = jnp.maximum(hidden + b_in[pl.ds(t, 1)], 0.0).astype(jnp.bfloat16)
            halves = jnp.dot(hidden, split, preferred_element_type=jnp.float32)
            centred = halves[:, :lat] + halves[:, lat:]
            squares = (centred * centred).astype(jnp.bfloat16)
            variance = jnp.dot(squares, ones, preferred_element_type=jnp.float32) * (1.0 / lat)
            normed = centred * lax.rsqrt(variance + 1e-05) * ln_gain[pl.ds(t, 1)]
            updated = (h.astype(jnp.float32) + normed).reshape(chunk, rows, lat)
            block = c * chunk + lax.broadcasted_iota(jnp.int32, (chunk, rows, lat), 0)
            updated = jnp.where(block < live, updated, 0.0).astype(out.dtype)
            if t == steps - 1:
                out[at] = updated
                stored(c).start()
            else:
                held[t + 1][at] = updated
                pools[t + 1][at] = updated
            return 0

        lax.fori_loop(0, n_fine // chunk, update, 0)
        if t < steps - 1:
            gather_dom(t + 1)
            start_dom(t + 1)
            gather_sub(t + 1)
            start_sub(t + 1)
            local_pool(t + 1)

    for t in range(steps):
        finish_halo_sends(t)
    for c in range(n_fine // chunk):
        stored(c).wait()

    peers(lambda to, other: coarse_copy(to, other, me).wait_send())


def per_device(
    n_dom,
    n_sub,
    fine_latent,
    coarse_latent,
    adj_index,
    adj_weight,
    interp_slot,
    interp_weight,
    coarse_send,
    halo_sub_send,
    halo_dom_send,
    block_count,
    w_in,
    b_in,
    w_out,
    ln_gain,
):
    n = n_dom * n_sub
    steps = w_in.shape[0]
    n_fine, rows, lat = fine_latent.shape
    slots = coarse_send.shape[2]
    hs, hd = halo_sub_send.shape[2], halo_dom_send.shape[2]
    pool = n_fine + n_sub * hs + 2 * hd
    kind = fine_latent.dtype

    def vmem(*lead):
        return pltpu.VMEM(lead + (rows, lat), kind)

    dma = pltpu.SemaphoreType.DMA
    scratch = (
        [vmem(n_fine)] * steps
        + [vmem(pool)] * steps
        + [vmem(n_sub, hs)] * steps
        + [vmem(2, hd)] * steps
        + [
            pltpu.VMEM(coarse_latent.shape, kind),
            pltpu.VMEM(adj_weight.shape, kind),
            pltpu.VMEM(interp_weight.shape, kind),
            vmem(n, slots),
            vmem(n * slots),
            vmem(n_fine),
            vmem(n_fine),
            pltpu.VMEM(w_in.shape, w_in.dtype),
            pltpu.VMEM(b_in.shape, b_in.dtype),
            pltpu.VMEM(w_out.shape, w_out.dtype),
            pltpu.VMEM(ln_gain.shape, ln_gain.dtype),
            dma((8,)),
            vmem(n_fine),
            dma((n_fine,)),
            dma((n,)),
            dma((n,)),
            dma((steps, n_sub)),
            dma((steps, n_sub)),
            dma((steps, 2)),
            dma((steps, 2)),
        ]
    )
    smem = pl.BlockSpec(memory_space=pltpu.SMEM)
    hbm = pl.BlockSpec(memory_space=pl.ANY)
    return pl.pallas_call(
        functools.partial(kernel, n_dom, n_sub, steps),
        out_shape=jax.ShapeDtypeStruct(fine_latent.shape, kind),
        in_specs=[smem] * 6 + [hbm] * 8,
        out_specs=hbm,
        scratch_shapes=scratch,
        compiler_params=pltpu.CompilerParams(
            collective_id=0, has_side_effects=True, vmem_limit_bytes=67043328
        ),
        name="graph_steps",
    )(
        adj_index.T,
        interp_slot.T,
        coarse_send.transpose(0, 2, 1),
        halo_sub_send,
        halo_dom_send,
        block_count.reshape(1, 1),
        fine_latent,
        coarse_latent,
        adj_weight,
        interp_weight,
        w_in,
        b_in,
        w_out,
        ln_gain,
    )


def solution(mesh):
    placed = (
        P(("dom", "sub"), None, None),
        P(("dom", "sub"), None, None),
        P(("dom", "sub"), None),
        P(("dom", "sub"), None, None),
        P(("dom", "sub"), None),
        P(("dom", "sub"), None, None),
        P(("dom", "sub"), None, None),
        P(("dom", "sub"), None, None),
        P(("dom", "sub"), None, None),
        P(("dom", "sub")),
        P(),
        P(),
        P(),
        P(),
    )
    return jax.shard_map(
        functools.partial(per_device, mesh.shape["dom"], mesh.shape["sub"]),
        mesh=mesh,
        in_specs=placed,
        out_specs=P(("dom", "sub"), None, None),
        check_vma=False,
    )
```

profile of v0, /device:TPU:9, one launch (start us, length us, event | category | flops | bytes accessed | tf_op | source)
XLA Modules:
  0.0 36.6 jit_solution(2075730201975874253)
XLA Ops:
  0.7 34.1 %graph_steps.1 = bf16[32,64,128]{2,1,0:T(8,128)(2,1)} custom-call(s32[16,32]{1,0:T(8,128)} %bitcast.5, s32[4,32]{1,0:T(4,128)} %bitcast.6, s32[1,1,32]{2,1,0:T(1,128)} %bitcast.7, s32[1,4,4]{2,1,0:T(4,128)} %halo_sub_send.1, s32[1,2,8]{2,1,0:T(2,128)} %halo_dom_send.1, s32[1,1]{1,0:T(1,128)} %bitcast.4.block_count, bf16[32,64,128]{2,1,0:T(8,128)(2,1)} %fine_hbm.1, ...), custom_call_target="tpu_custom_call" | custom-call | tf_op jit(solution)/shard_map/graph_steps/pallas_call | solution.py:366
  34.8 1.9 %copy.17 = bf16[32,64,128]{2,1,0:T(8,128)(2,1)} copy(bf16[32,64,128]{2,1,0:T(8,128)(2,1)} %graph_steps.1) | data formatting | bytes 1048576
where the time goes:
time: 36.9 us; the launch traced here: 36.6 us
  Pallas kernels  34.1 us (92%)
  local copies, waits for them, and re-layouts  1.87 us (5%)
  between operations  0.66 us (2%)
    pallas_call x1, Pallas kernels, per_device(): pl.pallas_call(functools.partial(kernel, n_dom, n_sub, steps), out_shape=...  34.1 us
    unnamed x1, local copies, waits for them, and re-layouts  1.87 us

commit v1 on v0

v1 whole, which is shorter than its diff:
```python
import functools
import math

import jax
import jax.numpy as jnp
from jax import lax
from jax.experimental import pallas as pl
from jax.experimental.pallas import tpu as pltpu
from jax.sharding import PartitionSpec as P

MESH = pl.DeviceIdType.MESH


def kernel(
    n_dom,
    n_sub,
    width,
    steps,
    fine_hbm,
    coarse_hbm,
    adj_index_hbm,
    adj_hbm,
    interp_slot_hbm,
    interp_hbm,
    coarse_send_hbm,
    halo_sub_hbm,
    halo_dom_hbm,
    count_hbm,
    w_in_hbm,
    b_in_hbm,
    w_out_hbm,
    ln_gain_hbm,
    out,
    *scratch,
):
    held = scratch[:steps]
    pools = scratch[steps : 2 * steps]
    sub_outs = scratch[2 * steps : 3 * steps]
    dom_outs = scratch[3 * steps : 4 * steps]
    (
        coarse,
        adj,
        iw,
        coarse_out,
        received,
        interp,
        summed,
        partial,
        w_in,
        b_in,
        w_out,
        ln_gain,
        adj_index,
        interp_slot,
        coarse_send,
        halo_sub_send,
        halo_dom_send,
        block_count,
        load_sem,
        ready,
        c_send,
        c_recv,
        s_send,
        s_recv,
        d_send,
        d_recv,
    ) = scratch[4 * steps :]

    n = n_dom * n_sub
    layers = n_dom // width
    dom, sub = lax.axis_index("dom"), lax.axis_index("sub")
    layer, column = dom // width, dom % width
    me = dom * n_sub + sub
    n_fine, rows, lat = out.shape
    slots = coarse_out.shape[1]
    hs = sub_outs[0].shape[1]
    hd = dom_outs[0].shape[1]
    k_a, k_i = adj_index.shape[0], interp_slot.shape[0]

    barrier = pltpu.get_barrier_semaphore()

    def wrapped(position, size):
        return jnp.where(position >= size, position - size, position)

    subs = [wrapped(sub + o, n_sub) for o in range(n_sub)]
    columns = [wrapped(column + o, width) for o in range(width)]

    def greet(to, other):
        pl.semaphore_signal(barrier, inc=1, device_id=(to, other), device_id_type=MESH)

    edges = [(layer < layers - 1, dom + width), (layer > 0, dom - width)]
    if width > 1:
        edges += [
            (jnp.logical_and(column == width - 1, dom < n_dom - 1), dom + 1),
            (jnp.logical_and(column == 0, dom > 0), dom - 1),
        ]

    for there, to in edges:

        @pl.when(there)
        def _(to=to):
            greet(to, sub)

    for c in range(width):
        for s in range(n_sub):
            if c or s:
                greet(layer * width + columns[c], subs[s])
    greeted = width * n_sub - 1
    for there, _ in edges:
        greeted = greeted + jnp.where(there, 1, 0)

    loads = [
        pltpu.make_async_copy(src, dst, load_sem.at[i])
        for i, (src, dst) in enumerate(
            [
                (fine_hbm, held[0]),
                (halo_dom_hbm, halo_dom_send),
                (halo_sub_hbm, halo_sub_send),
                (coarse_send_hbm, coarse_send),
                (coarse_hbm, coarse),
                (adj_index_hbm, adj_index),
                (interp_slot_hbm, interp_slot),
                (count_hbm, block_count),
                (adj_hbm, adj),
                (interp_hbm, iw),
                (w_in_hbm, w_in),
                (b_in_hbm, b_in),
                (w_out_hbm, w_out),
                (ln_gain_hbm, ln_gain),
            ]
        )
    ]
    for copy in loads[:8]:
        copy.start()

    def gather_sub(t):
        for i in range(n_sub):
            for s in range(hs):
                sub_outs[t][i, s] = held[t][halo_sub_send[0, i, s]]

    def gather_dom(t):
        for i in range(2):
            for s in range(hd):
                dom_outs[t][i, s] = held[t][halo_dom_send[0, i, s]]

    def sub_copy(t, peer, owner):
        return pltpu.make_async_remote_copy(
            src_ref=sub_outs[t].at[peer],
            dst_ref=pools[t].at[pl.ds(n_fine + owner * hs, hs)],
            send_sem=s_send.at[t],
            recv_sem=s_recv.at[t],
            device_id=(dom, peer),
            device_id_type=MESH,
        )

    def dom_copy(t, way):
        target = dom + 1 if way == 0 else dom - 1
        return pltpu.make_async_remote_copy(
            src_ref=dom_outs[t].at[way],
            dst_ref=pools[t].at[pl.ds(n_fine + n_sub * hs + way * hd, hd)],
            send_sem=d_send.at[t, way],
            recv_sem=d_recv.at[t, way],
            device_id=(target, sub),
            device_id_type=MESH,
        )

    def coarse_copy(to, other):
        return pltpu.make_async_remote_copy(
            src_ref=coarse_out.at[to * n_sub + other],
            dst_ref=received.at[pl.ds(me * slots, slots)],
            send_sem=c_send,
            recv_sem=c_recv,
            device_id=(to, other),
            device_id_type=MESH,
        )

    def all_of(ref, blocks, sem):
        part = ref.at[pl.ds(0, blocks)]
        return pltpu.make_async_copy(part, part, sem)

    def start_dom(t, way):
        @pl.when(dom < n_dom - 1 if way == 0 else dom > 0)
        def _():
            dom_copy(t, way).start()

    def start_sub(t):
        for o in range(1, n_sub):
            sub_copy(t, subs[o], sub).start()

    def local_pool(t):
        pools[t][pl.ds(n_fine + sub * hs, hs)] = sub_outs[t][sub]
        base = n_fine + n_sub * hs

        @pl.when(dom == 0)
        def _():
            pools[t][pl.ds(base, hd)] = jnp.zeros((hd, rows, lat), pools[t].dtype)

        @pl.when(dom == n_dom - 1)
        def _():
            pools[t][pl.ds(base + hd, hd)] = jnp.zeros((hd, rows, lat), pools[t].dtype)

    def wait_halo(t):
        all_of(pools[t], (n_sub - 1) * hs, s_recv.at[t]).wait()

        @pl.when(dom > 0)
        def _():
            dom_copy(t, 0).wait_recv()

        @pl.when(dom < n_dom - 1)
        def _():
            dom_copy(t, 1).wait_recv()

    def finish_halo_sends(t):
        all_of(pools[t], (n_sub - 1) * hs, s_send.at[t]).wait()

        @pl.when(dom < n_dom - 1)
        def _():
            dom_copy(t, 0).wait_send()

        @pl.when(dom > 0)
        def _():
            dom_copy(t, 1).wait_send()

    with jax.named_scope("A_load"):
        for copy in loads[:3]:
            copy.wait()
        gather_dom(0)
    with jax.named_scope("B_barrier"):
        pl.semaphore_wait(barrier, greeted)

    def tell(about):
        return lambda to: pl.semaphore_signal(
            ready.at[about], inc=1, device_id=(to, sub), device_id_type=MESH
        )

    @pl.when(layer < layers - 1)
    def _():
        tell(layer)(dom + width)

    @pl.when(layer > 0)
    def _():
        tell(layer)(dom - width)

    with jax.named_scope("C_halo"):
        start_dom(0, 0)
        start_dom(0, 1)
        gather_sub(0)
        start_sub(0)
    for copy in loads[8:]:
        copy.start()
    with jax.named_scope("D_gcoarse"):
        loads[3].wait()
        loads[4].wait()

        def gather_coarse(d, _):
            for s in range(slots):
                coarse_out[d, s] = coarse[coarse_send[0, s, d]]
            return 0

        lax.fori_loop(0, n, gather_coarse, 0, unroll=4)
        received[pl.ds(me * slots, slots)] = coarse_out[me]

    def send_layer(to_layer, skip):
        for c in range(width):
            for s in range(n_sub):
                if c or s or not skip:
                    coarse_copy(to_layer * width + columns[c], subs[s]).start()

    with jax.named_scope("E_ready"):
        for k in range(1, layers):

            @pl.when(layer >= k)
            def _():
                pl.semaphore_wait(ready.at[layer - k], 1)

                @pl.when(layer < layers - 1)
                def _():
                    tell(layer - k)(dom + width)

                send_layer(layer - k, False)

            @pl.when(layer + k < layers)
            def _():
                pl.semaphore_wait(ready.at[layer + k], 1)

                @pl.when(layer > 0)
                def _():
                    tell(layer + k)(dom - width)

                send_layer(layer + k, False)

        send_layer(layer, True)

    for copy in loads[5:8]:
        copy.wait()
    pools[0][pl.ds(0, n_fine)] = held[0][...]
    local_pool(0)

    live = block_count[0]
    chunk = math.gcd(n_fine, 16)

    def matmul(x, w):
        return jnp.dot(x, w, preferred_element_type=jnp.float32)

    def product(weights, table, index, tiles, b):
        picked = jnp.concatenate([table[index[k, b]] for k in range(tiles)], axis=0)
        return matmul(weights[b], picked).astype(jnp.bfloat16)

    def flat(ref, at):
        return ref[at].reshape(-1, lat)

    def second_layer(t):
        wide = w_out[t].astype(jnp.float32)
        wide = wide - jnp.mean(wide, axis=-1, keepdims=True)
        high = wide.astype(jnp.bfloat16)
        low = (wide - high.astype(jnp.float32)).astype(jnp.bfloat16)
        return jnp.concatenate([high, low], axis=1)

    def finish(t, h, hidden, split):
        ones = jnp.ones((lat, lat), jnp.bfloat16)
        hidden = jnp.maximum(hidden, 0.0).astype(jnp.bfloat16)
        halves = matmul(hidden, split)
        centred = halves[:, :lat] + halves[:, lat:]
        squares = (centred * centred).astype(jnp.bfloat16)
        variance = matmul(squares, ones) * (1.0 / lat)
        normed = centred * lax.rsqrt(variance + 1e-05) * ln_gain[pl.ds(t, 1)]
        return h.astype(jnp.float32) + normed

    def alive(updated, c):
        shape = (chunk, rows, lat)
        block = c * chunk + lax.broadcasted_iota(jnp.int32, shape, 0)
        updated = updated.reshape(shape)
        return jnp.where(block < live, updated, 0.0).astype(out.dtype)

    def chunks(body):
        def step(c, _):
            body(c, pl.ds(c * chunk, chunk))
            return 0

        lax.fori_loop(0, n_fine // chunk, step, 0)

    for t in range(steps):
        with jax.named_scope("F_weights"):
            if t == 0:
                for copy in loads[10:]:
                    copy.wait()
            split = second_layer(t)
            w_own = w_in[t, :lat]
            w_sum = w_in[t, lat : 2 * lat]
            w_interp = w_in[t, 2 * lat :]
            w_ends = jnp.concatenate([w_own, w_interp], axis=0)
            bias = b_in[pl.ds(t, 1)]
        if t > 0:
            with jax.named_scope("G_pre"):

                def before(c, at):
                    ends = jnp.concatenate([flat(held[t], at), flat(interp, at)], axis=1)
                    partial[at] = (matmul(ends, w_ends) + bias).reshape(chunk, rows, lat)

                chunks(before)
        with jax.named_scope("H_waithalo"):
            wait_halo(t)
            if t == 0:
                loads[8].wait()
        with jax.named_scope("I_product"):

            def gathered(c, at):
                for u in range(chunk):
                    b = c * chunk + u
                    summed[b] = product(adj, pools[t], adj_index, k_a, b)
                if t == 0:
                    ends = jnp.concatenate([flat(held[t], at), flat(summed, at)], axis=1)
                    w_first = w_in[t, : 2 * lat]
                    partial[at] = (matmul(ends, w_first) + bias).reshape(chunk, rows, lat)
                else:
                    hidden = flat(partial, at) + matmul(flat(summed, at), w_sum)
                    updated = alive(finish(t, flat(held[t], at), hidden, split), c)
                    if t == steps - 1:
                        out[at] = updated
                    else:
                        held[t + 1][at] = updated

            chunks(gathered)
        if t == 0:
            with jax.named_scope("J_waitcoarse"):
                loads[9].wait()
                all_of(received, (n - 1) * slots, c_recv).wait()
            if steps > 1:
                with jax.named_scope("K_early"):
                    for way in range(2):
                        picks = [halo_dom_send[0, way, s] for s in range(hd)]
                        mixed = jnp.concatenate(
                            [product(iw, received, interp_slot, k_i, g) for g in picks]
                        )
                        hidden = jnp.concatenate([partial[g] for g in picks])
                        own = jnp.concatenate([held[0][g] for g in picks])
                        updated = finish(0, own, hidden + matmul(mixed, w_interp), split)
                        for s, g in enumerate(picks):
                            one = updated[s * rows : (s + 1) * rows]
                            one = jnp.where(g < live, one, 0.0)
                            dom_outs[1][way, s] = one.astype(out.dtype)
                        start_dom(1, way)
            with jax.named_scope("L_update"):

                def interpolated(c, at):
                    for u in range(chunk):
                        b = c * chunk + u
                        interp[b] = product(iw, received, interp_slot, k_i, b)
                    hidden = flat(partial, at) + matmul(flat(interp, at), w_interp)
                    updated = alive(finish(t, flat(held[t], at), hidden, split), c)
                    if steps == 1:
                        out[at] = updated
                    else:
                        held[1][at] = updated

                chunks(interpolated)
        if t < steps - 1:
            with jax.named_scope("M_send"):
                if t > 0:
                    gather_dom(t + 1)
                    start_dom(t + 1, 0)
                    start_dom(t + 1, 1)
                gather_sub(t + 1)
                start_sub(t + 1)
                pools[t + 1][pl.ds(0, n_fine)] = held[t + 1][...]
                local_pool(t + 1)

    with jax.named_scope("N_finish"):
        for t in range(steps):
            finish_halo_sends(t)
        all_of(received, (n - 1) * slots, c_send).wait()


def per_device(
    n_dom,
    n_sub,
    fine_latent,
    coarse_latent,
    adj_index,
    adj_weight,
    interp_slot,
    interp_weight,
    coarse_send,
    halo_sub_send,
    halo_dom_send,
    block_count,
    w_in,
    b_in,
    w_out,
    ln_gain,
):
    n = n_dom * n_sub
    width = max(w for w in range(1, n_dom + 1) if n_dom % w == 0 and w * w <= n_dom)
    steps = w_in.shape[0]
    n_fine, rows, lat = fine_latent.shape
    slots = coarse_send.shape[2]
    hs, hd = halo_sub_send.shape[2], halo_dom_send.shape[2]
    pool = n_fine + n_sub * hs + 2 * hd
    kind = fine_latent.dtype

    def vmem(*lead):
        return pltpu.VMEM(lead + (rows, lat), kind)

    dma = pltpu.SemaphoreType.DMA
    args = (
        fine_latent,
        coarse_latent,
        adj_index.T,
        adj_weight,
        interp_slot.T,
        interp_weight,
        coarse_send.transpose(0, 2, 1),
        halo_sub_send,
        halo_dom_send,
        block_count,
        w_in,
        b_in,
        w_out,
        ln_gain,
    )
    scratch = (
        [vmem(n_fine)] * steps
        + [vmem(pool)] * steps
        + [vmem(n_sub, hs)] * steps
        + [vmem(2, hd)] * steps
        + [
            pltpu.VMEM(coarse_latent.shape, kind),
            pltpu.VMEM(adj_weight.shape, kind),
            pltpu.VMEM(interp_weight.shape, kind),
            vmem(n, slots),
            vmem(n * slots),
            vmem(n_fine),
            vmem(n_fine),
            pltpu.VMEM((n_fine, rows, lat), jnp.float32),
            pltpu.VMEM(w_in.shape, w_in.dtype),
            pltpu.VMEM(b_in.shape, b_in.dtype),
            pltpu.VMEM(w_out.shape, w_out.dtype),
            pltpu.VMEM(ln_gain.shape, ln_gain.dtype),
        ]
        + [pltpu.SMEM(args[i].shape, jnp.int32) for i in (2, 4, 6, 7, 8, 9)]
        + [
            dma((14,)),
            pltpu.SemaphoreType.REGULAR((n_dom // width,)),
            dma,
            dma,
            dma((steps,)),
            dma((steps,)),
            dma((steps, 2)),
            dma((steps, 2)),
        ]
    )
    hbm = pl.BlockSpec(memory_space=pltpu.HBM)
    return pl.pallas_call(
        functools.partial(kernel, n_dom, n_sub, width, steps),
        out_shape=pltpu.VMEM(fine_latent.shape, kind),
        in_specs=[hbm] * 14,
        scratch_shapes=scratch,
        compiler_params=pltpu.CompilerParams(
            collective_id=0, has_side_effects=True, vmem_limit_bytes=67043328 - fine_latent.size * 2
        ),
        name="graph_steps",
    )(*args)


def solution(mesh):
    placed = (
        P(("dom", "sub"), None, None),
        P(("dom", "sub"), None, None),
        P(("dom", "sub"), None),
        P(("dom", "sub"), None, None),
        P(("dom", "sub"), None),
        P(("dom", "sub"), None, None),
        P(("dom", "sub"), None, None),
        P(("dom", "sub"), None, None),
        P(("dom", "sub"), None, None),
        P(("dom", "sub")),
        P(),
        P(),
        P(),
        P(),
    )
    return jax.shard_map(
        functools.partial(per_device, mesh.shape["dom"], mesh.shape["sub"]),
        mesh=mesh,
        in_specs=placed,
        out_specs=P(("dom", "sub"), None, None),
        check_vma=False,
    )
```

time: 36.9 us -> 33.3 us (0.902)
  the two profiles are of different devices: /device:TPU:9 before, /device:TPU:1 now
where the time goes in v1:
time: 33.3 us; the launch traced here: 32.8 us
  Pallas kernels  31.3 us (94%)
  local copies, waits for them, and re-layouts  0.8 us (2%)
  between operations  0.66 us (2%)
    pallas_call x1, Pallas kernels, per_device(): pl.pallas_call(functools.partial(kernel, n_dom, n_sub, width, steps), out...  31.3 us
    unnamed x1, local copies, waits for them, and re-layouts  0.8 us

profile of v1, /device:TPU:1, one launch (start us, length us, event | category | flops | bytes accessed | tf_op | source)
XLA Modules:
  0.0 32.8 jit_solution(1082006441591129427)
XLA Ops:
  0.7 31.3 %graph_steps.1 = bf16[32,64,128]{2,1,0:T(8,128)(2,1)S(1)} custom-call(bf16[32,64,128]{2,1,0:T(8,128)(2,1)} %fine_hbm.1, bf16[8,64,128]{2,1,0:T(8,128)(2,1)} %coarse_hbm.1, s32[16,32]{1,0:T(8,128)} %bitcast.3, bf16[32,64,1024]{2,1,0:T(8,128)(2,1)} %adj_hbm.1, s32[4,32]{1,0:T(4,128)} %bitcast.4, bf16[32,64,256]{2,1,0:T(8,128)(2,1)} %interp_hbm.1, ...), custom_call_target="tpu_custom_call" | custom-call | tf_op jit(solution)/shard_map/graph_steps/pallas_call | solution.py:513
  32.0 0.8 %copy.16 = bf16[32,64,128]{2,1,0:T(8,128)(2,1)} copy(bf16[32,64,128]{2,1,0:T(8,128)(2,1)S(1)} %graph_steps.1) | data formatting | bytes 1048576

commit v2 on v1

--- a/solution.py
+++ b/solution.py
@@ -43,6 +43,8 @@
         iw,
         coarse_out,
         received,
+        relay_in,
+        relay_out,
         interp,
         summed,
         partial,
@@ -56,8 +58,11 @@
         halo_sub_send,
         halo_dom_send,
         block_count,
+        relay_send,
         load_sem,
         ready,
+        r_send,
+        r_recv,
         c_send,
         c_recv,
         s_send,
@@ -68,6 +73,7 @@
 
     n = n_dom * n_sub
     layers = n_dom // width
+    middle = layers // 2
     dom, sub = lax.axis_index("dom"), lax.axis_index("sub")
     layer, column = dom // width, dom % width
     me = dom * n_sub + sub
@@ -174,9 +180,50 @@
             device_id_type=MESH,
         )
 
+    low, high = layer == middle - 1, layer == middle
+    mate = jnp.where(low, dom + width, dom - width)
+    mated = mate * n_sub + sub
+
+    def relay_copies():
+        pairs = [(coarse, relay_in), (coarse_send, relay_send)]
+        return [
+            pltpu.make_async_remote_copy(
+                src_ref=src,
+                dst_ref=dst,
+                send_sem=r_send.at[i],
+                recv_sem=r_recv.at[i],
+                device_id=(mate, sub),
+                device_id_type=MESH,
+            )
+            for i, (src, dst) in enumerate(pairs)
+        ]
+
+    def passed_on(to, other):
+        peer = to * n_sub + other
+        return pltpu.make_async_remote_copy(
+            src_ref=relay_out.at[peer],
+            dst_ref=received.at[pl.ds(mated * slots, slots)],
+            send_sem=c_send,
+            recv_sem=c_recv,
+            device_id=(to, other),
+            device_id_type=MESH,
+        )
+
     def all_of(ref, blocks, sem):
         part = ref.at[pl.ds(0, blocks)]
         return pltpu.make_async_copy(part, part, sem)
+
+    def coarse_wait(sem, blocks_low, blocks_high):
+        cases = [(low, blocks_low), (high, blocks_high)]
+        for case, blocks in cases if middle else []:
+
+            @pl.when(case)
+            def _():
+                all_of(received, blocks * slots, sem).wait()
+
+        @pl.when(jnp.logical_not(jnp.logical_or(low, high)) if middle else n > 0)
+        def _():
+            all_of(received, (n - 1) * slots, sem).wait()
 
     def start_dom(t, way):
         @pl.when(dom < n_dom - 1 if way == 0 else dom > 0)
@@ -242,6 +289,14 @@
         tell(layer)(dom - width)
 
     with jax.named_scope("C_halo"):
+        loads[3].wait()
+        loads[4].wait()
+
+        @pl.when(jnp.logical_or(low, high))
+        def _():
+            for copy in relay_copies():
+                copy.start()
+
         start_dom(0, 0)
         start_dom(0, 1)
         gather_sub(0)
@@ -249,8 +304,6 @@
     for copy in loads[8:]:
         copy.start()
     with jax.named_scope("D_gcoarse"):
-        loads[3].wait()
-        loads[4].wait()
 
         def gather_coarse(d, _):
             for s in range(slots):
@@ -260,11 +313,18 @@
         lax.fori_loop(0, n, gather_coarse, 0, unroll=4)
         received[pl.ds(me * slots, slots)] = coarse_out[me]
 
-    def send_layer(to_layer, skip):
+    def send_layer(to_layer, skip, copy):
         for c in range(width):
             for s in range(n_sub):
                 if c or s or not skip:
-                    coarse_copy(to_layer * width + columns[c], subs[s]).start()
+                    copy(to_layer * width + columns[c], subs[s]).start()
+
+    def direct(to_layer):
+        across = jnp.where(to_layer < middle, high, low)
+
+        @pl.when(jnp.logical_not(across))
+        def _():
+            send_layer(to_layer, False, coarse_copy)
 
     with jax.named_scope("E_ready"):
         for k in range(1, layers):
@@ -277,7 +337,7 @@
                 def _():
                     tell(layer - k)(dom + width)
 
-                send_layer(layer - k, False)
+                direct(layer - k)
 
             @pl.when(layer + k < layers)
             def _():
@@ -287,9 +347,37 @@
                 def _():
                     tell(layer + k)(dom - width)
 
-                send_layer(layer + k, False)
-
-        send_layer(layer, True)
+                direct(layer + k)
+
+        send_layer(layer, True, coarse_copy)
+
+    half = width * n_sub
+
+    def relay(first, last):
+        for copy in relay_copies():
+            copy.wait_recv()
+
+        def gather_relay(d, _):
+            for s in range(slots):
+                relay_out[d, s] = relay_in[relay_send[0, s, d]]
+            return 0
+
+        lax.fori_loop(first * half, last * half, gather_relay, 0, unroll=4)
+        for away in range(1, last - first):
+            send_layer(layer + away if first else layer - away, False, passed_on)
+        send_layer(layer, True, passed_on)
+        received[pl.ds(mated * slots, slots)] = relay_out[me]
+
+    with jax.named_scope("F_relay"):
+        if middle:
+
+            @pl.when(low)
+            def _():
+                relay(0, middle)
+
+            @pl.when(high)
+            def _():
+                relay(middle, layers)
 
     for copy in loads[5:8]:
         copy.wait()
@@ -384,22 +472,30 @@
         if t == 0:
             with jax.named_scope("J_waitcoarse"):
                 loads[9].wait()
-                all_of(received, (n - 1) * slots, c_recv).wait()
+                coarse_wait(c_recv, n - 2, n - 2)
             if steps > 1:
                 with jax.named_scope("K_early"):
-                    for way in range(2):
-                        picks = [halo_dom_send[0, way, s] for s in range(hd)]
+                    def early(picks):
                         mixed = jnp.concatenate(
                             [product(iw, received, interp_slot, k_i, g) for g in picks]
                         )
                         hidden = jnp.concatenate([partial[g] for g in picks])
                         own = jnp.concatenate([held[0][g] for g in picks])
                         updated = finish(0, own, hidden + matmul(mixed, w_interp), split)
-                        for s, g in enumerate(picks):
-                            one = updated[s * rows : (s + 1) * rows]
-                            one = jnp.where(g < live, one, 0.0)
-                            dom_outs[1][way, s] = one.astype(out.dtype)
+                        for i, g in enumerate(picks):
+                            one = updated[i * rows : (i + 1) * rows]
+                            yield jnp.where(g < live, one, 0.0).astype(out.dtype)
+
+                    for way in range(2):
+                        picks = [halo_dom_send[0, way, s] for s in range(hd)]
+                        for s, one in enumerate(early(picks)):
+                            dom_outs[1][way, s] = one
                         start_dom(1, way)
+                    places = [(subs[o], s) for o in range(1, n_sub) for s in range(hs)]
+                    picks = [halo_sub_send[0, peer, s] for peer, s in places]
+                    for (peer, s), one in zip(places, early(picks)):
+                        sub_outs[1][peer, s] = one
+                    start_sub(1)
             with jax.named_scope("L_update"):
 
                 def interpolated(c, at):
@@ -420,15 +516,24 @@
                     gather_dom(t + 1)
                     start_dom(t + 1, 0)
                     start_dom(t + 1, 1)
-                gather_sub(t + 1)
-                start_sub(t + 1)
+                if t > 0:
+                    gather_sub(t + 1)
+                    start_sub(t + 1)
+                else:
+                    for s in range(hs):
+                        sub_outs[1][sub, s] = held[1][halo_sub_send[0, sub, s]]
                 pools[t + 1][pl.ds(0, n_fine)] = held[t + 1][...]
                 local_pool(t + 1)
 
     with jax.named_scope("N_finish"):
         for t in range(steps):
             finish_halo_sends(t)
-        all_of(received, (n - 1) * slots, c_send).wait()
+        coarse_wait(c_send, 2 * middle * half - 2, 2 * (layers - middle) * half - 2)
+
+        @pl.when(jnp.logical_or(low, high))
+        def _():
+            for copy in relay_copies():
+                copy.wait_send()
 
 
 def per_device(
@@ -489,6 +594,8 @@
             pltpu.VMEM(interp_weight.shape, kind),
             vmem(n, slots),
             vmem(n * slots),
+            pltpu.VMEM(coarse_latent.shape, kind),
+            vmem(n, slots),
             vmem(n_fine),
             vmem(n_fine),
             pltpu.VMEM((n_fine, rows, lat), jnp.float32),
@@ -497,10 +604,12 @@
             pltpu.VMEM(w_out.shape, w_out.dtype),
             pltpu.VMEM(ln_gain.shape, ln_gain.dtype),
         ]
-        + [pltpu.SMEM(args[i].shape, jnp.int32) for i in (2, 4, 6, 7, 8, 9)]
+        + [pltpu.SMEM(args[i].shape, jnp.int32) for i in (2, 4, 6, 7, 8, 9, 6)]
         + [
             dma((14,)),
             pltpu.SemaphoreType.REGULAR((n_dom // width,)),
+            dma((2,)),
+            dma((2,)),
             dma,
             dma,
             dma((steps,)),

time: 33.3 us -> 30.7 us (0.922)
  the two profiles are of different devices: /device:TPU:1 before, /device:TPU:0 now
where the time goes in v2:
time: 30.7 us; the launch traced here: 30.6 us
  Pallas kernels  29.1 us (95%)
  local copies, waits for them, and re-layouts  0.8 us (3%)
  between operations  0.66 us (2%)
    pallas_call x1, Pallas kernels, per_device(): pl.pallas_call(functools.partial(kernel, n_dom, n_sub, width, steps), out...  29.1 us
    unnamed x1, local copies, waits for them, and re-layouts  0.8 us

profile of v2, /device:TPU:0, one launch (start us, length us, event | category | flops | bytes accessed | tf_op | source)
XLA Modules:
  0.0 30.6 jit_solution(14029740392903792463)
XLA Ops:
  0.7 29.1 %graph_steps.1 = bf16[32,64,128]{2,1,0:T(8,128)(2,1)S(1)} custom-call(bf16[32,64,128]{2,1,0:T(8,128)(2,1)} %fine_hbm.1, bf16[8,64,128]{2,1,0:T(8,128)(2,1)} %coarse_hbm.1, s32[16,32]{1,0:T(8,128)} %bitcast.3, bf16[32,64,1024]{2,1,0:T(8,128)(2,1)} %adj_hbm.1, s32[4,32]{1,0:T(4,128)} %bitcast.4, bf16[32,64,256]{2,1,0:T(8,128)(2,1)} %interp_hbm.1, ...), custom_call_target="tpu_custom_call" | custom-call | tf_op jit(solution)/shard_map/graph_steps/pallas_call | solution.py:622
  29.8 0.8 %copy.16 = bf16[32,64,128]{2,1,0:T(8,128)(2,1)} copy(bf16[32,64,128]{2,1,0:T(8,128)(2,1)S(1)} %graph_steps.1) | data formatting | bytes 1048576

commit v3 on v2

--- a/solution.py
+++ b/solution.py
@@ -46,7 +46,6 @@
         relay_in,
         relay_out,
         interp,
-        summed,
         partial,
         w_in,
         b_in,
@@ -160,7 +159,7 @@
         )
 
     def dom_copy(t, way):
-        target = dom + 1 if way == 0 else dom - 1
+        target = dom + 1 - 2 * way
         return pltpu.make_async_remote_copy(
             src_ref=dom_outs[t].at[way],
             dst_ref=pools[t].at[pl.ds(n_fine + n_sub * hs + way * hd, hd)],
@@ -226,7 +225,7 @@
             all_of(received, (n - 1) * slots, sem).wait()
 
     def start_dom(t, way):
-        @pl.when(dom < n_dom - 1 if way == 0 else dom > 0)
+        @pl.when(jnp.where(way == 0, dom < n_dom - 1, dom > 0))
         def _():
             dom_copy(t, way).start()
 
@@ -267,6 +266,9 @@
         @pl.when(dom > 0)
         def _():
             dom_copy(t, 1).wait_send()
+
+    first_way = jnp.where(column == 0, 1, 0)
+    ways = [first_way, 1 - first_way]
 
     with jax.named_scope("A_load"):
         for copy in loads[:3]:
@@ -297,8 +299,8 @@
             for copy in relay_copies():
                 copy.start()
 
-        start_dom(0, 0)
-        start_dom(0, 1)
+        for way in ways:
+            start_dom(0, way)
         gather_sub(0)
         start_sub(0)
     for copy in loads[8:]:
@@ -313,18 +315,20 @@
         lax.fori_loop(0, n, gather_coarse, 0, unroll=4)
         received[pl.ds(me * slots, slots)] = coarse_out[me]
 
-    def send_layer(to_layer, skip, copy):
-        for c in range(width):
+    def send(to_layer, which, copy, skip=False):
+        for c in which:
             for s in range(n_sub):
                 if c or s or not skip:
                     copy(to_layer * width + columns[c], subs[s]).start()
 
-    def direct(to_layer):
+    def direct(to_layer, which):
         across = jnp.where(to_layer < middle, high, low)
 
         @pl.when(jnp.logical_not(across))
         def _():
-            send_layer(to_layer, False, coarse_copy)
+            send(to_layer, which, coarse_copy)
+
+    here, aside = range(1), range(1, width)
 
     with jax.named_scope("E_ready"):
         for k in range(1, layers):
@@ -337,7 +341,7 @@
                 def _():
                     tell(layer - k)(dom + width)
 
-                direct(layer - k)
+                direct(layer - k, here)
 
             @pl.when(layer + k < layers)
             def _():
@@ -347,9 +351,20 @@
                 def _():
                     tell(layer + k)(dom - width)
 
-                direct(layer + k)
-
-        send_layer(layer, True, coarse_copy)
+                direct(layer + k, here)
+
+        for k in reversed(range(1, layers)):
+
+            @pl.when(layer >= k)
+            def _():
+                direct(layer - k, aside)
+
+            @pl.when(layer + k < layers)
+            def _():
+                direct(layer + k, aside)
+
+        send(layer, here, coarse_copy, True)
+        send(layer, aside, coarse_copy)
 
     half = width * n_sub
 
@@ -363,9 +378,10 @@
             return 0
 
         lax.fori_loop(first * half, last * half, gather_relay, 0, unroll=4)
-        for away in range(1, last - first):
-            send_layer(layer + away if first else layer - away, False, passed_on)
-        send_layer(layer, True, passed_on)
+        for which in (here, aside):
+            for away in range(1, last - first):
+                send(layer + away if first else layer - away, which, passed_on)
+            send(layer, which, passed_on, which is here)
         received[pl.ds(mated * slots, slots)] = relay_out[me]
 
     with jax.named_scope("F_relay"):
@@ -404,19 +420,33 @@
         low = (wide - high.astype(jnp.float32)).astype(jnp.bfloat16)
         return jnp.concatenate([high, low], axis=1)
 
-    def finish(t, h, hidden, split):
+    def activate(hidden):
+        return jnp.maximum(hidden, 0.0).astype(jnp.bfloat16)
+
+    def centre(hidden, split):
+        halves = matmul(hidden, split)
+        return halves[:, :lat] + halves[:, lat:]
+
+    def normalize(t, h, centred):
         ones = jnp.ones((lat, lat), jnp.bfloat16)
-        hidden = jnp.maximum(hidden, 0.0).astype(jnp.bfloat16)
-        halves = matmul(hidden, split)
-        centred = halves[:, :lat] + halves[:, lat:]
         squares = (centred * centred).astype(jnp.bfloat16)
         variance = matmul(squares, ones) * (1.0 / lat)
         normed = centred * lax.rsqrt(variance + 1e-05) * ln_gain[pl.ds(t, 1)]
         return h.astype(jnp.float32) + normed
 
-    def alive(updated, c):
-        shape = (chunk, rows, lat)
-        block = c * chunk + lax.broadcasted_iota(jnp.int32, shape, 0)
+    def finish(t, h, hidden, split):
+        return normalize(t, h, centre(activate(hidden), split))
+
+    def staggered(pieces, stages):
+        held_back = {}
+        for i in range(len(pieces) + len(stages) - 1):
+            for s, stage in enumerate(stages):
+                if 0 <= i - s < len(pieces):
+                    held_back[i - s] = stage(pieces[i - s], held_back.get(i - s))
+
+    def alive(updated, first):
+        shape = (updated.shape[0] // rows, rows, lat)
+        block = first + lax.broadcasted_iota(jnp.int32, shape, 0)
         updated = updated.reshape(shape)
         return jnp.where(block < live, updated, 0.0).astype(out.dtype)
 
@@ -452,23 +482,39 @@
                 loads[8].wait()
         with jax.named_scope("I_product"):
 
-            def gathered(c, at):
-                for u in range(chunk):
-                    b = c * chunk + u
-                    summed[b] = product(adj, pools[t], adj_index, k_a, b)
-                if t == 0:
-                    ends = jnp.concatenate([flat(held[t], at), flat(summed, at)], axis=1)
-                    w_first = w_in[t, : 2 * lat]
-                    partial[at] = (matmul(ends, w_first) + bias).reshape(chunk, rows, lat)
+            size = math.gcd(n_fine, 4 if t == 0 else 4)
+            pieces = range(0, n_fine, size)
+
+            def gathered(first, _):
+                blocks = range(first, first + size)
+                total = [product(adj, pools[t], adj_index, k_a, b) for b in blocks]
+                return jnp.concatenate(total, axis=0)
+
+            def started(first, total):
+                at = pl.ds(first, size)
+                ends = jnp.concatenate([flat(held[t], at), total], axis=1)
+                hidden = matmul(ends, w_in[t, : 2 * lat]) + bias
+                partial[at] = hidden.reshape(size, rows, lat)
+
+            def activated(first, total):
+                at = pl.ds(first, size)
+                return activate(flat(partial, at) + matmul(total, w_sum))
+
+            def centred(first, hidden):
+                return centre(hidden, split)
+
+            def updated(first, values):
+                at = pl.ds(first, size)
+                values = alive(normalize(t, flat(held[t], at), values), first)
+                if t == steps - 1:
+                    out[at] = values
                 else:
-                    hidden = flat(partial, at) + matmul(flat(summed, at), w_sum)
-                    updated = alive(finish(t, flat(held[t], at), hidden, split), c)
-                    if t == steps - 1:
-                        out[at] = updated
-                    else:
-                        held[t + 1][at] = updated
-
-            chunks(gathered)
+                    held[t + 1][at] = values
+
+            if t == 0:
+                staggered(pieces, [gathered, started])
+            else:
+                staggered(pieces, [gathered, activated, centred, updated])
         if t == 0:
             with jax.named_scope("J_waitcoarse"):
                 loads[9].wait()
@@ -486,7 +532,7 @@
                             one = updated[i * rows : (i + 1) * rows]
                             yield jnp.where(g < live, one, 0.0).astype(out.dtype)
 
-                    for way in range(2):
+                    for way in ways:
                         picks = [halo_dom_send[0, way, s] for s in range(hd)]
                         for s, one in enumerate(early(picks)):
                             dom_outs[1][way, s] = one
@@ -503,7 +549,8 @@
                         b = c * chunk + u
                         interp[b] = product(iw, received, interp_slot, k_i, b)
                     hidden = flat(partial, at) + matmul(flat(interp, at), w_interp)
-                    updated = alive(finish(t, flat(held[t], at), hidden, split), c)
+                    updated = finish(t, flat(held[t], at), hidden, split)
+                    updated = alive(updated, c * chunk)
                     if steps == 1:
                         out[at] = updated
                     else:
@@ -514,8 +561,8 @@
             with jax.named_scope("M_send"):
                 if t > 0:
                     gather_dom(t + 1)
-                    start_dom(t + 1, 0)
-                    start_dom(t + 1, 1)
+                    for way in ways:
+                        start_dom(t + 1, way)
                 if t > 0:
                     gather_sub(t + 1)
                     start_sub(t + 1)
@@ -596,7 +643,6 @@
             vmem(n * slots),
             pltpu.VMEM(coarse_latent.shape, kind),
             vmem(n, slots),
-            vmem(n_fine),
             vmem(n_fine),
             pltpu.VMEM((n_fine, rows, lat), jnp.float32),
             pltpu.VMEM(w_in.shape, w_in.dtype),

time: 30.7 us -> 29.6 us (0.964)
  the two profiles are of different devices: /device:TPU:0 before, /device:TPU:1 now
where the time goes in v3:
time: 29.6 us; the launch traced here: 29.5 us
  Pallas kernels  28 us (95%)
  local copies, waits for them, and re-layouts  0.8 us (3%)
  between operations  0.66 us (2%)
    pallas_call x1, Pallas kernels, per_device(): pl.pallas_call(functools.partial(kernel, n_dom, n_sub, width, steps), out...  28 us
    unnamed x1, local copies, waits for them, and re-layouts  0.8 us

profile of v3, /device:TPU:1, one launch (start us, length us, event | category | flops | bytes accessed | tf_op | source)
XLA Modules:
  0.0 29.5 jit_solution(17072565548221719279)
XLA Ops:
  0.7 28.0 %graph_steps.1 = bf16[32,64,128]{2,1,0:T(8,128)(2,1)S(1)} custom-call(bf16[32,64,128]{2,1,0:T(8,128)(2,1)} %fine_hbm.1, bf16[8,64,128]{2,1,0:T(8,128)(2,1)} %coarse_hbm.1, s32[16,32]{1,0:T(8,128)} %bitcast.3, bf16[32,64,1024]{2,1,0:T(8,128)(2,1)} %adj_hbm.1, s32[4,32]{1,0:T(4,128)} %bitcast.4, bf16[32,64,256]{2,1,0:T(8,128)(2,1)} %interp_hbm.1, ...), custom_call_target="tpu_custom_call" | custom-call | tf_op jit(solution)/shard_map/graph_steps/pallas_call | solution.py:668
  28.7 0.8 %copy.16 = bf16[32,64,128]{2,1,0:T(8,128)(2,1)} copy(bf16[32,64,128]{2,1,0:T(8,128)(2,1)S(1)} %graph_steps.1) | data formatting | bytes 1048576

commit v4 on v3

--- a/solution.py
+++ b/solution.py
@@ -115,7 +115,7 @@
         greeted = greeted + jnp.where(there, 1, 0)
 
     loads = [
-        pltpu.make_async_copy(src, dst, load_sem.at[i])
+        pltpu.make_async_copy(src, dst, load_sem.at[i % 8])
         for i, (src, dst) in enumerate(
             [
                 (fine_hbm, held[0]),
@@ -303,6 +303,8 @@
             start_dom(0, way)
         gather_sub(0)
         start_sub(0)
+    for copy in loads[5:8]:
+        copy.wait()
     for copy in loads[8:]:
         copy.start()
     with jax.named_scope("D_gcoarse"):
@@ -395,8 +397,6 @@
             def _():
                 relay(middle, layers)
 
-    for copy in loads[5:8]:
-        copy.wait()
     pools[0][pl.ds(0, n_fine)] = held[0][...]
     local_pool(0)
 
@@ -428,9 +428,7 @@
         return halves[:, :lat] + halves[:, lat:]
 
     def normalize(t, h, centred):
-        ones = jnp.ones((lat, lat), jnp.bfloat16)
-        squares = (centred * centred).astype(jnp.bfloat16)
-        variance = matmul(squares, ones) * (1.0 / lat)
+        variance = jnp.mean(centred * centred, axis=-1, keepdims=True)
         normed = centred * lax.rsqrt(variance + 1e-05) * ln_gain[pl.ds(t, 1)]
         return h.astype(jnp.float32) + normed
 
@@ -652,7 +650,7 @@
         ]
         + [pltpu.SMEM(args[i].shape, jnp.int32) for i in (2, 4, 6, 7, 8, 9, 6)]
         + [
-            dma((14,)),
+            dma((8,)),
             pltpu.SemaphoreType.REGULAR((n_dom // width,)),
             dma((2,)),
             dma((2,)),

time: 29.6 us -> 29.3 us (0.990)
  Pallas kernels: 28 us -> 27.7 us
    pallas_call x1, Pallas kernels: 28 us -> 27.7 us  [per_device(): pl.pallas_call(functools.partial(kernel, n_dom, n_sub, width, steps), out...]
where the time goes in v4:
time: 29.3 us; the launch traced here: 29.1 us
  Pallas kernels  27.7 us (95%)
  local copies, waits for them, and re-layouts  0.8 us (3%)
  between operations  0.66 us (2%)
    pallas_call x1, Pallas kernels, per_device(): pl.pallas_call(functools.partial(kernel, n_dom, n_sub, width, steps), out...  27.7 us
    unnamed x1, local copies, waits for them, and re-layouts  0.8 us

profile of v4, /device:TPU:1, one launch (start us, length us, event | category | flops | bytes accessed | tf_op | source)
XLA Modules:
  0.0 29.1 jit_solution(12117941004102106938)
XLA Ops:
  0.7 27.7 %graph_steps.1 = bf16[32,64,128]{2,1,0:T(8,128)(2,1)S(1)} custom-call(bf16[32,64,128]{2,1,0:T(8,128)(2,1)} %fine_hbm.1, bf16[8,64,128]{2,1,0:T(8,128)(2,1)} %coarse_hbm.1, s32[16,32]{1,0:T(8,128)} %bitcast.3, bf16[32,64,1024]{2,1,0:T(8,128)(2,1)} %adj_hbm.1, s32[4,32]{1,0:T(4,128)} %bitcast.4, bf16[32,64,256]{2,1,0:T(8,128)(2,1)} %interp_hbm.1, ...), custom_call_target="tpu_custom_call" | custom-call | tf_op jit(solution)/shard_map/graph_steps/pallas_call | solution.py:666
  28.3 0.8 %copy.16 = bf16[32,64,128]{2,1,0:T(8,128)(2,1)} copy(bf16[32,64,128]{2,1,0:T(8,128)(2,1)S(1)} %graph_steps.1) | data formatting | bytes 1048576
